TPU v7x, 256 devices: a whole 4x4x8 slice. The times are simulated.
256 devices in a mesh: frame: 64 (over z, x, core), slab: 4 (over y).
Axes of the slice: x: 4, y: 4, z: 8, core: 2. Of those that a mesh axis runs over, the one named last changes fastest.
Arguments:
- latents: bfloat16 [128, 16, 160, 512], P('frame', 'slab'), may hold values from -20 to 20
- clip_starts: int32 [128], replicated, may hold values from 0 to 1
- w_space: bfloat16 [3, 3, 512, 512], replicated, may hold values from -0.09375 to 0.09375
- w_time: bfloat16 [3, 512, 512], replicated, may hold values from -0.15625 to 0.15625
- w_qkv: bfloat16 [512, 1536], replicated, may hold values from -0.25 to 0.25
- w_out: bfloat16 [512, 512], replicated, may hold values from -0.25 to 0.25
Outputs:
- block_out: bfloat16 [128, 16, 160, 512], P('frame', 'slab')
All inputs are finite; a program needn't handle non-finite values.
Results may differ from a plain program's by a relative error of at most 0.0065.
Values may be sent and summed in bfloat16 or wider, within the bound.
No kernel may reach another device: no remote copies, remote signals or barrier semaphores. Data moves between devices by JAX's collectives and lax.ppermute only.
A program may use at most 64 MiB of HBM per device.

v0:
```python
import functools

import jax
import jax.numpy as jnp
from jax import lax
from jax.experimental import pallas as pl
from jax.experimental.pallas import tpu as pltpu
from jax.sharding import Mesh
from jax.sharding import PartitionSpec as P

HEADS = 8
FRAME = ("frame_0", "frame_1", "frame_2")
BF = jnp.bfloat16
F32 = jnp.float32
COLS = 160
CH = 512
PAIR = 2 * COLS
TOTAL = 128
VMEM = pl.BlockSpec(memory_space=pltpu.VMEM)
ANY = pl.BlockSpec(memory_space=pl.ANY)
HBM = pl.BlockSpec(memory_space=pltpu.HBM)


def far(x):
    return pltpu.with_memory_space_constraint(x, pltpu.HBM)
PARAMS = pltpu.CompilerParams(vmem_limit_bytes=20 * 1024 * 1024)


def dot(a, b):
    return jnp.dot(a, b, preferred_element_type=F32)


def dot_t(a, b):
    return lax.dot_general(a, b, (((1,), (1,)), ((), ())), preferred_element_type=F32)


def iotas(rows, cols):
    i = lax.broadcasted_iota(jnp.int32, (rows, cols), 0)
    j = lax.broadcasted_iota(jnp.int32, (rows, cols), 1)
    return i, j


def one_hot(hit):
    return jnp.where(hit, 1.0, 0.0).astype(BF)


def row_source(i):
    head = i < 256
    tail = i - 256
    g = jnp.where(head, i >> 4, tail >> 2)
    k = jnp.where(head, (i >> 1) & 7, 8 + ((tail >> 1) & 1))
    return (i & 1) * COLS + 10 * g + k


def pack_matrix():
    i, j = iotas(PAIR, PAIR)
    return one_hot(row_source(i) == j)


def unpack_matrix():
    i, j = iotas(PAIR, PAIR)
    return one_hot(row_source(j) == i)


def fold_source(i):
    return ((i >> 2) & 3) * 64 + (i >> 4) * 4 + (i & 3)


def fold_matrix():
    i, j = iotas(256, 256)
    return one_hot(fold_source(i) == j)


def unfold_matrix():
    i, j = iotas(256, 256)
    return one_hot(fold_source(j) == i)


def lanes(x, l):
    return x[:, l * 128 : (l + 1) * 128]


def pack_row(y, pack, fold, store):
    p = dot(pack, y).astype(BF)
    for l in range(4):
        store(16 * l, lanes(p[:256], l).reshape(16, 16, 128))
    tail = jnp.concatenate([lanes(p[256:], l) for l in range(4)], axis=0)
    store(64, dot(fold, tail).astype(BF).reshape(16, 16, 128))


def silu(v):
    return v / (1.0 + jnp.exp(-v))


def spread(x, store):
    wide = x.astype(F32)
    i, _ = iotas(COLS, CH)
    before = jnp.where(i == 0, 0.0, pltpu.roll(wide, 1, 0))
    after = jnp.where(i == COLS - 1, 0.0, pltpu.roll(wide, COLS - 1, 0))
    store(0, before.astype(BF))
    store(1, x)
    store(2, after.astype(BF))


def spread_into(ref, first, x):
    def store(b, v):
        ref[pl.ds(first, COLS), pl.ds(b * CH, CH)] = v

    spread(x, store)


def conv_inner_kernel(x_ref, w_any, out_ref, edge_ref, outer_ref, xs, pay, mid_tap, sem, sems):
    taps = (outer_ref.at[0], mid_tap, outer_ref.at[1])
    order = (1, 2, 0)
    weights = fetch([w_any.at[a] for a in order], [taps[a] for a in order], sems)
    for r in range(4):
        for f in range(2):
            spread_into(xs, r * PAIR + f * COLS, x_ref[f, r])
    pack, fold = pack_matrix(), fold_matrix()

    def tap(r, a):
        return dot(xs[pl.ds((r + a - 1) * PAIR, PAIR), :], taps[a][...])

    weights[0].wait()
    weights[1].wait()
    edge_ref[0] = tap(0, 1) + tap(0, 2)
    weights[2].wait()

    for r in (1, 2):
        y = silu(tap(r, 0) + tap(r, 1) + tap(r, 2)).astype(BF)

        def store(first, tiles, r=r):
            pay[pl.ds((r - 1) * 16, 16), pl.ds(first, 16), :] = tiles

        pack_row(y, pack, fold, store)
    copy = pltpu.make_async_copy(pay, out_ref.at[pl.ds(16, 32)], sem)
    copy.start()
    edge_ref[1] = tap(3, 0) + tap(3, 1)
    copy.wait()


def conv_edge_kernel(low_ref, high_ref, edge_ref, w_ref, held_ref, out_ref, xs, pay, sem):
    del held_ref
    for f in range(2):
        spread_into(xs, f * COLS, low_ref[f, 0])
        spread_into(xs, PAIR + f * COLS, high_ref[f, 0])
    pack, fold = pack_matrix(), fold_matrix()
    for n in range(2):
        y = silu(edge_ref[n] + dot(xs[pl.ds(n * PAIR, PAIR), :], w_ref[n])).astype(BF)

        def store(first, tiles, n=n):
            pay[n, :, pl.ds(first, 16), :] = tiles

        pack_row(y, pack, fold, store)
    copies = [
        pltpu.make_async_copy(pay.at[n], out_ref.at[pl.ds(48 * n, 16)], sem.at[n]) for n in range(2)
    ]
    for copy in copies:
        copy.start()
    for copy in copies:
        copy.wait()


def conv(latents, low, high, w_space):
    taps = far(w_space.reshape(3, 3 * CH, CH))
    payload = jax.ShapeDtypeStruct((64, 80, 128), BF)
    started, edge, outer = pl.pallas_call(
        conv_inner_kernel,
        out_shape=(
            payload,
            jax.ShapeDtypeStruct((2, PAIR, CH), F32),
            jax.ShapeDtypeStruct((2, 3 * CH, CH), BF),
        ),
        in_specs=[VMEM, HBM],
        out_specs=(ANY, VMEM, VMEM),
        scratch_shapes=[
            pltpu.VMEM((4 * PAIR, 3 * CH), BF),
            pltpu.VMEM((32, 80, 128), BF),
            pltpu.VMEM((3 * CH, CH), BF),
            pltpu.SemaphoreType.DMA,
            pltpu.SemaphoreType.DMA((3,)),
        ],
        compiler_params=PARAMS,
        cost_estimate=pl.CostEstimate(
            flops=2 * 10 * PAIR * 3 * CH * CH, bytes_accessed=10 << 20, transcendentals=0
        ),
        name="conv_inner",
    )(latents, taps)
    return pl.pallas_call(
        conv_edge_kernel,
        out_shape=payload,
        in_specs=[VMEM, VMEM, VMEM, VMEM, ANY],
        out_specs=ANY,
        scratch_shapes=[
            pltpu.VMEM((2 * PAIR, 3 * CH), BF),
            pltpu.VMEM((2, 16, 80, 128), BF),
            pltpu.SemaphoreType.DMA((2,)),
        ],
        input_output_aliases={4: 0},
        compiler_params=PARAMS,
        name="conv_edge",
    )(low, high, edge, outer, started)


def gather_a(i):
    return ((i >> 1) & 7) * 16 + (i >> 4) * 2 + (i & 1)


def gather_b(i):
    return ((i >> 1) & 7) * 16 + (i >> 5) * 4 + ((i >> 4) & 1) * 2 + (i & 1)


def fetch(sources, buffers, sems):
    copies = [
        pltpu.make_async_copy(source, buffer, sems.at[n])
        for n, (source, buffer) in enumerate(zip(sources, buffers))
    ]
    for copy in copies:
        copy.start()
    return copies


def middle_kernel(
    x_ref, shift_ref, bias_ref, wt_any, wq_any, wo_any, out_ref,
    xs, mixed, qkv, att, res, wt_ref, wq_ref, wo_ref, sems,
):
    weights = fetch((wt_any, wq_any, wo_any), (wt_ref, wq_ref, wo_ref), sems)
    i, j = iotas(128, 128)
    take_a, take_b = one_hot(gather_a(i) == j), one_hot(gather_b(i) == j)
    give_a, give_b = one_hot(gather_a(j) == i), one_hot(gather_b(j) == i)
    for n in range(8):
        part = jnp.concatenate(
            [x_ref[pl.ds(8 * n, 8), pl.ds(16 * l, 16), :].reshape(128, 128) for l in range(4)],
            axis=1,
        )
        rows = dot(take_a, part).astype(BF)
        for k in range(8):
            xs[pl.ds(k * TOTAL + 16 * n, 16), pl.ds(0, CH)] = rows[16 * k : 16 * k + 16]
        rows = dot(take_b, x_ref[pl.ds(8 * n, 8), pl.ds(64, 16), :].reshape(128, 128)).astype(BF)
        for l in range(4):
            for k in range(2):
                at = (2 * l + k) * 16
                xs[pl.ds((8 + k) * TOTAL + 16 * n, 16), pl.ds(128 * l, 128)] = rows[at : at + 16]
    shift = shift_ref[...]
    for k in range(10):
        moved = dot(shift, xs[pl.ds(k * TOTAL, TOTAL), pl.ds(0, CH)]).astype(BF)
        xs[pl.ds(k * TOTAL, TOTAL), pl.ds(CH, CH)] = moved[:TOTAL]
        xs[pl.ds(k * TOTAL, TOTAL), pl.ds(2 * CH, CH)] = moved[TOTAL:]
    weights[0].wait()
    weights[1].wait()
    for c in range(2):
        part = pl.ds(640 * c, 640)
        mixed[part, :] = dot(xs[part, :], wt_ref[...]).astype(BF)
        for t in range(3):
            cut = pl.ds(t * CH, CH)
            qkv[part, cut] = dot(mixed[part, :], wq_ref[:, cut]).astype(BF)

    bias = bias_ref[...]
    _, lane = iotas(TOTAL, 128)
    left = jnp.where(lane < 64, 1.0, 0.0).astype(BF)
    right = jnp.where(lane < 64, 0.0, 1.0).astype(BF)
    scale = BF(0.125)
    weigh = jnp.concatenate([left, right], axis=0)

    def pixel(k, carry):
        rows = pl.ds(pl.multiple_of(k * TOTAL, TOTAL), TOTAL)
        for h in range(4):
            q = qkv[rows, pl.ds(128 * h, 128)]
            key = qkv[rows, pl.ds(CH + 128 * h, 128)]
            v = qkv[rows, pl.ds(2 * CH + 128 * h, 128)]
            keys = jnp.concatenate([key * (left * scale), key * (right * scale)], axis=0)
            s = dot_t(q, keys)
            p = []
            for t in range(2):
                part = lanes(s, t) + bias
                p.append(jnp.exp(part - jnp.max(part, axis=-1, keepdims=True)).astype(BF))
            values = jnp.concatenate([jnp.concatenate([v * left, v * right], axis=0), weigh], axis=1)
            o = dot(jnp.concatenate(p, axis=1), values)
            att[rows, pl.ds(128 * h, 128)] = (o[:, :128] / o[:, 128:]).astype(BF)
        return carry

    lax.fori_loop(0, 10, pixel, 0, unroll=10)
    weights[2].wait()
    for c in range(2):
        part = pl.ds(640 * c, 640)
        res[part, :] = dot(att[part, :], wo_ref[...]).astype(BF)
    for n in range(8):
        rows = jnp.concatenate(
            [res[pl.ds(k * TOTAL + 16 * n, 16), :] for k in range(8)], axis=0
        )
        part = dot(give_a, rows).astype(BF)
        for l in range(4):
            out_ref[pl.ds(8 * n, 8), pl.ds(16 * l, 16), :] = lanes(part, l).reshape(8, 16, 128)
        rows = jnp.concatenate(
            [
                res[pl.ds((8 + k) * TOTAL + 16 * n, 16), pl.ds(128 * l, 128)]
                for l in range(4)
                for k in range(2)
            ],
            axis=0,
        )
        out_ref[pl.ds(8 * n, 8), pl.ds(64, 16), :] = dot(give_b, rows).astype(BF).reshape(8, 16, 128)


def middle(arrived, clip_starts, w_time, w_qkv, w_out):
    clip_ids = jnp.cumsum(clip_starts)
    same = clip_ids[None, :] == clip_ids[:, None]
    i, j = iotas(TOTAL, TOTAL)
    bias = jnp.where(same & (j <= i), 0.0, -1e30).astype(F32)
    shift = jnp.concatenate([one_hot(same & (j == i - 1)), one_hot(same & (j == i - 2))], axis=0)
    return pl.pallas_call(
        middle_kernel,
        out_shape=jax.ShapeDtypeStruct((64, 80, 128), BF),
        in_specs=[VMEM] * 3 + [HBM] * 3,
        out_specs=VMEM,
        scratch_shapes=[
            pltpu.VMEM((1280, 3 * CH), BF),
            pltpu.VMEM((1280, CH), BF),
            pltpu.VMEM((1280, 3 * CH), BF),
            pltpu.VMEM((1280, CH), BF),
            pltpu.VMEM((1280, CH), BF),
            pltpu.VMEM((3 * CH, CH), BF),
            pltpu.VMEM((CH, 3 * CH), BF),
            pltpu.VMEM((CH, CH), BF),
            pltpu.SemaphoreType.DMA((3,)),
        ],
        compiler_params=PARAMS,
        name="middle",
    )(arrived, shift, bias, far(w_time.reshape(3 * CH, CH)), far(w_qkv), far(w_out))


def finish_kernel(x_ref, latent_ref, out_ref):
    unpack, unfold = unpack_matrix(), unfold_matrix()
    head = jnp.concatenate(
        [x_ref[:, pl.ds(16 * l, 16), :].reshape(256, 128) for l in range(4)], axis=1
    )
    tail = dot(unfold, x_ref[:, pl.ds(64, 16), :].reshape(256, 128)).astype(BF)
    tail = jnp.concatenate([tail[64 * l : 64 * l + 64] for l in range(4)], axis=1)
    y = dot(unpack, jnp.concatenate([head, tail], axis=0))
    for f in range(2):
        part = y[f * COLS : (f + 1) * COLS]
        out_ref[f, 0] = (latent_ref[f, 0].astype(F32) + part).astype(BF)


def finish(returned, latents):
    block = pl.BlockSpec((2, 1, COLS, CH), lambda r: (0, r, 0, 0))
    return pl.pallas_call(
        finish_kernel,
        out_shape=jax.ShapeDtypeStruct(latents.shape, BF),
        grid=(4,),
        in_specs=[pl.BlockSpec((16, 80, 128), lambda r: (r, 0, 0)), block],
        out_specs=block,
        compiler_params=PARAMS,
        name="finish",
    )(returned, latents)


def on_device(latents, clip_starts, w_space, w_time, w_qkv, w_out):
    count = lax.axis_size("slab")
    forward = [(i, i + 1) for i in range(count - 1)]
    backward = [(target, source) for source, target in forward]
    low = lax.ppermute(latents[:, 3:], "slab", forward)
    high = lax.ppermute(latents[:, :1], "slab", backward)
    payload = conv(latents, low, high, w_space)
    arrived = lax.all_to_all(payload, FRAME, split_axis=0, concat_axis=0, tiled=True)
    result = middle(arrived, clip_starts, w_time, w_qkv, w_out)
    returned = lax.all_to_all(result, FRAME, split_axis=0, concat_axis=0, tiled=True)
    return finish(returned, latents)


def solution(mesh):
    finer = Mesh(
        mesh.devices.reshape(8, 4, 2, mesh.shape["slab"]), ("frame_0", "frame_1", "frame_2", "slab")
    )
    return jax.shard_map(
        on_device,
        mesh=finer,
        in_specs=(P(FRAME, "slab", None, None), P(), P(), P(), P(), P()),
        out_specs=P(FRAME, "slab", None, None),
        check_vma=False,
    )
```

profile of v0, /device:TPU:8, one launch (start us, length us, event | category | flops | bytes accessed | tf_op | source)
XLA Modules:
  0.0 118.2 jit_solution(13939184823157116049)
XLA Ops:
  0.0 0.0 copy-start
  0.0 1.2 %fusion.1 = (bf16[2,1,160,512]{3,2,1,0:T(8,128)(2,1)S(1)}, bf16[2,1,160,512]{3,2,1,0:T(8,128)(2,1)S(1)}) fusion(bf16[2,4,160,512]{3,2,1,0:T(8,128)(2,1)} %latent_ref.1), kind=kLoop, calls=%fused_computation.12 | loop fusion | bytes 1310720 | tf_op jit(solution)/shard_map/slice | solution.py:363
  1.2 3.5 %collective-permute-start = (bf16[2,1,160,512]{3,2,1,0:T(8,128)(2,1)S(1)}, bf16[2,1,160,512]{3,2,1,0:T(8,128)(2,1)S(1)}, u32[]{:S(2)}, u32[]{:S(2)}) collective-permute-start(bf16[2,1,160,512]{3,2,1,0:T(8,128)(2,1)S(1)} %get-tuple-element.12), channel_id=1, source_target_pairs={{0,1},{1,2},{2,3},{4,5},{5,6},{6,7},{8,9},{9,10},{10,11},{12,13},{... | collective-permute-start | bytes 983048 | tf_op jit(solution)/shard_map/ppermute | solution.py:362
  4.7 2.4 %collective-permute-start.1 = (bf16[2,1,160,512]{3,2,1,0:T(8,128)(2,1)S(1)}, bf16[2,1,160,512]{3,2,1,0:T(8,128)(2,1)S(1)}, u32[]{:S(2)}, u32[]{:S(2)}) collective-permute-start(bf16[2,1,160,512]{3,2,1,0:T(8,128)(2,1)S(1)} %get-tuple-element.11), channel_id=1, source_target_pairs={{1,0},{2,1},{3,2},{5,4},{6,5},{7,6},{9,8},{10,9},{11,10},{13,12},{... | collective-permute-start | bytes 983048 | tf_op jit(solution)/shard_map/ppermute | solution.py:363
  7.1 0.0 copy-done
  7.1 8.4 %conv_inner.1 = (bf16[64,80,128]{2,1,0:T(8,128)(2,1)}, f32[2,320,512]{2,1,0:T(8,128)S(1)}, bf16[2,1536,512]{2,1,0:T(8,128)(2,1)S(1)}) custom-call(bf16[2,4,160,512]{3,2,1,0:T(8,128)(2,1)S(1)} %copy-done, bf16[3,1536,512]{2,1,0:T(8,128)(2,1)} %bitcast.5), custom_call_target="tpu_custom_call" | custom-call | flops 5033164800 | bytes 10485760 | tf_op jit(solution)/shard_map/conv_inner/pallas_call | solution.py:167
  15.5 0.0 collective-permute-done.low_ref
  15.5 0.3 collective-permute-done.1.high_ref
  15.8 3.1 %conv_edge.1 = bf16[64,80,128]{2,1,0:T(8,128)(2,1)} custom-call(bf16[2,1,160,512]{3,2,1,0:T(8,128)(2,1)S(1)} %collective-permute-done.low_ref, bf16[2,1,160,512]{3,2,1,0:T(8,128)(2,1)S(1)} %collective-permute-done.1.high_ref, f32[2,320,512]{2,1,0:T(8,128)S(1)} %get-tuple-element.8.edge_ref, ...), custom_call_target="tpu_custom_call", output_to_operand_aliasing={{}: (4, {})} | custom-call | tf_op jit(solution)/shard_map/conv_edge/pallas_call | solution.py:189
  18.9 0.0 copy-start.1
  18.9 12.1 %all-to-all-start = ((bf16[64,80,128]{2,1,0:T(8,128)(2,1)}), bf16[64,80,128]{2,1,0:T(8,128)(2,1)S(1)}, u32[]{:S(2)}, u32[]{:S(2)}) async-start(bf16[64,80,128]{2,1,0:T(8,128)(2,1)} %conv_edge.1), calls=%async_computation | async-start | bytes 2621440 | tf_op jit(solution)/shard_map/all_to_all | solution.py:365
  31.1 0.0 copy-done.1
  31.1 0.1 copy.9
  31.2 0.2 reduce-window.8
  31.3 0.1 reduce
  31.5 0.1 fusion
  31.6 33.7 %all-to-all-done.x_ref = bf16[64,80,128]{2,1,0:T(8,128)(2,1)S(1)} async-done(((bf16[64,80,128]{2,1,0:T(8,128)(2,1)}), bf16[64,80,128]{2,1,0:T(8,128)(2,1)S(1)}, u32[]{:S(2)}, u32[]{:S(2)}) %all-to-all-start) | async-done | bytes 1310752 | tf_op jit(solution)/shard_map/all_to_all | solution.py:365
  65.4 10.3 %middle.1 = bf16[64,80,128]{2,1,0:T(8,128)(2,1)S(1)} custom-call(bf16[64,80,128]{2,1,0:T(8,128)(2,1)S(1)} %all-to-all-done.x_ref, bf16[256,128]{1,0:T(8,128)(2,1)S(1)} %pad_maximum_fusion.shift_ref, f32[128,128]{1,0:T(8,128)S(1)} %get-tuple-element.13.bias_ref, bf16[1536,512]{1,0:T(8,128)(2,1)} %bitcast.3, bf16[512,1536]{1,0:T(8,128)(2,1)} %wq_any.1, ...), custom_call_target="tpu_custom_call" | custom-call | tf_op jit(solution)/shard_map/middle/pallas_call | solution.py:311
  75.7 39.8 %all_to_all.10.x_ref = bf16[64,80,128]{2,1,0:T(8,128)(2,1)S(1)} all-to-all(bf16[64,80,128]{2,1,0:T(8,128)(2,1)S(1)} %middle.1), channel_id=1, replica_groups=mesh['frame_0'=8,'frame_1'=4,'frame_2'=2,'slab'=4] {'frame_0','frame_1',..., dimensions={0} | all-to-all | bytes 2621440 | tf_op jit(solution)/shard_map/all_to_all | solution.py:367
  115.4 2.8 %finish.1 = bf16[2,4,160,512]{3,2,1,0:T(8,128)(2,1)} custom-call(bf16[64,80,128]{2,1,0:T(8,128)(2,1)S(1)} %all_to_all.10.x_ref, bf16[2,4,160,512]{3,2,1,0:T(8,128)(2,1)S(1)} %copy-done), custom_call_target="tpu_custom_call" | custom-call | tf_op jit(solution)/shard_map/finish/pallas_call | solution.py:347
  (2 shorter events, 0.0 us)
Async XLA Ops:
  0.0 7.1 %copy-start = (bf16[2,4,160,512]{3,2,1,0:T(8,128)(2,1)S(1)}, bf16[2,4,160,512]{3,2,1,0:T(8,128)(2,1)}, u32[]{:S(2)}) copy-start(bf16[2,4,160,512]{3,2,1,0:T(8,128)(2,1)} %latent_ref.1) | copy-start | bytes 3932164
  1.2 14.3 %collective-permute-start = (bf16[2,1,160,512]{3,2,1,0:T(8,128)(2,1)S(1)}, bf16[2,1,160,512]{3,2,1,0:T(8,128)(2,1)S(1)}, u32[]{:S(2)}, u32[]{:S(2)}) collective-permute-start(bf16[2,1,160,512]{3,2,1,0:T(8,128)(2,1)S(1)} %get-tuple-element.12), channel_id=1, source_target_pairs={{0,1},{1,2},{2,3},{4,5},{5,6},{6,7},{8,9},{9,10},{10,11},{12,13},{... | collective-permute-start | bytes 983048 | tf_op jit(solution)/shard_map/ppermute | solution.py:362
  4.7 11.1 %collective-permute-start.1 = (bf16[2,1,160,512]{3,2,1,0:T(8,128)(2,1)S(1)}, bf16[2,1,160,512]{3,2,1,0:T(8,128)(2,1)S(1)}, u32[]{:S(2)}, u32[]{:S(2)}) collective-permute-start(bf16[2,1,160,512]{3,2,1,0:T(8,128)(2,1)S(1)} %get-tuple-element.11), channel_id=1, source_target_pairs={{1,0},{2,1},{3,2},{5,4},{6,5},{7,6},{9,8},{10,9},{11,10},{13,12},{... | collective-permute-start | bytes 983048 | tf_op jit(solution)/shard_map/ppermute | solution.py:363
  18.9 12.1 %copy-start.1 = (s32[128]{0:T(128)S(1)}, s32[128]{0:T(128)}, u32[]{:S(2)}) copy-start(s32[128]{0:T(128)} %param.7) | copy-start | bytes 1540
  18.9 46.4 %all-to-all-start = ((bf16[64,80,128]{2,1,0:T(8,128)(2,1)}), bf16[64,80,128]{2,1,0:T(8,128)(2,1)S(1)}, u32[]{:S(2)}, u32[]{:S(2)}) async-start(bf16[64,80,128]{2,1,0:T(8,128)(2,1)} %conv_edge.1), calls=%async_computation | async-start | bytes 2621440 | tf_op jit(solution)/shard_map/all_to_all | solution.py:365
where the time goes:
time: 119 us; the launch traced here: 118 us
  blocking collectives  39.8 us (33%)
  waiting for transfers between devices  34 us (29%)
  Pallas kernels  24.6 us (21%)
  starting transfers between devices  18 us (15%)
  local copies, waits for them, and re-layouts  1.34 us (1%)
    all_to_all x1, blocking collectives, on_device(): lax.all_to_all(result, FRAME, split_axis=0, concat_axis=0, tiled=True)  39.8 us
    all_to_all x1, waiting for transfers between devices, on_device(): lax.all_to_all(payload, FRAME, split_axis=0, concat_axis=0, tiled=True)  33.7 us
    all_to_all x1, starting transfers between devices, on_device(): lax.all_to_all(payload, FRAME, split_axis=0, concat_axis=0, tiled=True)  12.1 us
    pallas_call x1, Pallas kernels, middle(): pl.pallas_call(middle_kernel, out_shape=jax.ShapeDtypeStruct((64, 80, 128...  10.3 us
    pallas_call x1, Pallas kernels, conv(): pl.pallas_call(conv_inner_kernel, out_shape=(payload, jax.ShapeDtypeStruc...  8.37 us
    ppermute x1, starting transfers between devices, on_device(): low = lax.ppermute(latents[:, 3:], 'slab', forward)  3.48 us
    pallas_call x1, Pallas kernels, conv(): pl.pallas_call(conv_edge_kernel, out_shape=payload, in_specs=[VMEM, VMEM,...  3.12 us
    pallas_call x1, Pallas kernels, finish(): pl.pallas_call(finish_kernel, out_shape=jax.ShapeDtypeStruct(latents.shap...  2.76 us
  transfers between devices with their start and end apart: 3, of which 2 were waited for; matrix products, arithmetic and copies ran while one was open for 0% of the time, Pallas kernels for 7%

commit v1 on v0

--- a/solution.py
+++ b/solution.py
@@ -44,48 +44,30 @@
     return jnp.where(hit, 1.0, 0.0).astype(BF)
 
 
-def row_source(i):
-    head = i < 256
-    tail = i - 256
-    g = jnp.where(head, i >> 4, tail >> 2)
-    k = jnp.where(head, (i >> 1) & 7, 8 + ((tail >> 1) & 1))
-    return (i & 1) * COLS + 10 * g + k
-
-
-def pack_matrix():
-    i, j = iotas(PAIR, PAIR)
-    return one_hot(row_source(i) == j)
-
-
-def unpack_matrix():
-    i, j = iotas(PAIR, PAIR)
-    return one_hot(row_source(j) == i)
-
-
-def fold_source(i):
-    return ((i >> 2) & 3) * 64 + (i >> 4) * 4 + (i & 3)
-
-
-def fold_matrix():
-    i, j = iotas(256, 256)
-    return one_hot(fold_source(i) == j)
-
-
-def unfold_matrix():
-    i, j = iotas(256, 256)
-    return one_hot(fold_source(j) == i)
+def tail_source(i):
+    return ((i >> 2) & 3) * 64 + (i & 1) * 32 + 2 * (i >> 4) + ((i >> 1) & 1)
 
 
 def lanes(x, l):
     return x[:, l * 128 : (l + 1) * 128]
 
 
-def pack_row(y, pack, fold, store):
-    p = dot(pack, y).astype(BF)
+def stack_lanes(x):
+    return jnp.concatenate([lanes(x, l) for l in range(4)], axis=0)
+
+
+def tail_matrix():
+    i, j = iotas(256, 256)
+    return one_hot(tail_source(i) == j)
+
+
+def pack_row(y, tail, store):
+    halves = [y[f * COLS : f * COLS + 128].reshape(16, 8, CH) for f in range(2)]
+    head = jnp.concatenate(halves, axis=1).astype(BF)
     for l in range(4):
-        store(16 * l, lanes(p[:256], l).reshape(16, 16, 128))
-    tail = jnp.concatenate([lanes(p[256:], l) for l in range(4)], axis=0)
-    store(64, dot(fold, tail).astype(BF).reshape(16, 16, 128))
+        store(16 * l, head[:, :, l * 128 : (l + 1) * 128])
+    rest = jnp.concatenate([y[f * COLS + 128 : (f + 1) * COLS] for f in range(2)], axis=0)
+    store(64, dot(tail, stack_lanes(rest.astype(BF))).astype(BF).reshape(16, 16, 128))
 
 
 def silu(v):
@@ -97,8 +79,8 @@
     i, _ = iotas(COLS, CH)
     before = jnp.where(i == 0, 0.0, pltpu.roll(wide, 1, 0))
     after = jnp.where(i == COLS - 1, 0.0, pltpu.roll(wide, COLS - 1, 0))
-    store(0, before.astype(BF))
-    store(1, x)
+    store(0, x)
+    store(1, before.astype(BF))
     store(2, after.astype(BF))
 
 
@@ -109,33 +91,52 @@
     spread(x, store)
 
 
-def conv_inner_kernel(x_ref, w_any, out_ref, edge_ref, outer_ref, xs, pay, mid_tap, sem, sems):
+def conv_inner_kernel(
+    x_ref, w_any, out_ref, edge_ref, outer_ref, xs, pay, pay_sum, mid_tap, sem, sems
+):
     taps = (outer_ref.at[0], mid_tap, outer_ref.at[1])
-    order = (1, 2, 0)
-    weights = fetch([w_any.at[a] for a in order], [taps[a] for a in order], sems)
+    order = [(a, b) for a in (1, 2, 0) for b in (1, 0, 2)]
+    spot = (1, 0, 2)
+    weights = fetch(
+        [w_any.at[a, pl.ds(b * CH, CH)] for a, b in order],
+        [taps[a].at[pl.ds(spot[b] * CH, CH)] for a, b in order],
+        sems,
+    )
+    weights[0].wait()
+    centre = []
+    for r in range(4):
+        x = jnp.concatenate([x_ref[0, r], x_ref[1, r]], axis=0)
+        centre.append(dot(x, mid_tap[pl.ds(0, CH), :]))
+    edge_ref[0] = centre[0]
+    edge_ref[1] = centre[3]
+    for n in range(2):
+        pay_sum[n] = centre[1 + n]
     for r in range(4):
         for f in range(2):
             spread_into(xs, r * PAIR + f * COLS, x_ref[f, r])
-    pack, fold = pack_matrix(), fold_matrix()
+    tail = tail_matrix()
 
     def tap(r, a):
         return dot(xs[pl.ds((r + a - 1) * PAIR, PAIR), :], taps[a][...])
 
-    weights[0].wait()
-    weights[1].wait()
-    edge_ref[0] = tap(0, 1) + tap(0, 2)
-    weights[2].wait()
-
+    def sides(r):
+        return dot(xs[pl.ds(r * PAIR, PAIR), pl.ds(CH, 2 * CH)], mid_tap[pl.ds(CH, 2 * CH), :])
+
+    for copy in weights[1:6]:
+        copy.wait()
+    edge_ref[0] = edge_ref[0] + sides(0) + tap(0, 2)
+    for copy in weights[6:]:
+        copy.wait()
     for r in (1, 2):
-        y = silu(tap(r, 0) + tap(r, 1) + tap(r, 2)).astype(BF)
+        y = silu(pay_sum[r - 1] + sides(r) + tap(r, 0) + tap(r, 2))
 
         def store(first, tiles, r=r):
             pay[pl.ds((r - 1) * 16, 16), pl.ds(first, 16), :] = tiles
 
-        pack_row(y, pack, fold, store)
+        pack_row(y, tail, store)
     copy = pltpu.make_async_copy(pay, out_ref.at[pl.ds(16, 32)], sem)
     copy.start()
-    edge_ref[1] = tap(3, 0) + tap(3, 1)
+    edge_ref[1] = edge_ref[1] + sides(3) + tap(3, 0)
     copy.wait()
 
 
@@ -144,19 +145,19 @@
     for f in range(2):
         spread_into(xs, f * COLS, low_ref[f, 0])
         spread_into(xs, PAIR + f * COLS, high_ref[f, 0])
-    pack, fold = pack_matrix(), fold_matrix()
+    tail = tail_matrix()
+    copies = []
     for n in range(2):
-        y = silu(edge_ref[n] + dot(xs[pl.ds(n * PAIR, PAIR), :], w_ref[n])).astype(BF)
+        y = silu(edge_ref[n] + dot(xs[pl.ds(n * PAIR, PAIR), :], w_ref[n]))
 
         def store(first, tiles, n=n):
             pay[n, :, pl.ds(first, 16), :] = tiles
 
-        pack_row(y, pack, fold, store)
-    copies = [
-        pltpu.make_async_copy(pay.at[n], out_ref.at[pl.ds(48 * n, 16)], sem.at[n]) for n in range(2)
-    ]
-    for copy in copies:
-        copy.start()
+        pack_row(y, tail, store)
+        copies.append(
+            pltpu.make_async_copy(pay.at[n], out_ref.at[pl.ds(48 * n, 16)], sem.at[n])
+        )
+        copies[n].start()
     for copy in copies:
         copy.wait()
 
@@ -176,9 +177,10 @@
         scratch_shapes=[
             pltpu.VMEM((4 * PAIR, 3 * CH), BF),
             pltpu.VMEM((32, 80, 128), BF),
+            pltpu.VMEM((2, PAIR, CH), F32),
             pltpu.VMEM((3 * CH, CH), BF),
             pltpu.SemaphoreType.DMA,
-            pltpu.SemaphoreType.DMA((3,)),
+            pltpu.SemaphoreType.DMA((9,)),
         ],
         compiler_params=PARAMS,
         cost_estimate=pl.CostEstimate(
@@ -203,7 +205,7 @@
 
 
 def gather_a(i):
-    return ((i >> 1) & 7) * 16 + (i >> 4) * 2 + (i & 1)
+    return ((i >> 1) & 7) * 16 + (i & 1) * 8 + (i >> 4)
 
 
 def gather_b(i):
@@ -329,27 +331,36 @@
     )(arrived, shift, bias, far(w_time.reshape(3 * CH, CH)), far(w_qkv), far(w_out))
 
 
-def finish_kernel(x_ref, latent_ref, out_ref):
-    unpack, unfold = unpack_matrix(), unfold_matrix()
-    head = jnp.concatenate(
-        [x_ref[:, pl.ds(16 * l, 16), :].reshape(256, 128) for l in range(4)], axis=1
-    )
-    tail = dot(unfold, x_ref[:, pl.ds(64, 16), :].reshape(256, 128)).astype(BF)
-    tail = jnp.concatenate([tail[64 * l : 64 * l + 64] for l in range(4)], axis=1)
-    y = dot(unpack, jnp.concatenate([head, tail], axis=0))
-    for f in range(2):
-        part = y[f * COLS : (f + 1) * COLS]
-        out_ref[f, 0] = (latent_ref[f, 0].astype(F32) + part).astype(BF)
+def finish_kernel(x_ref, latent_ref, out_any, out, sems):
+    i, j = iotas(256, 256)
+    spread_tail = one_hot(tail_source(j) == i)
+    copies = []
+    for r in range(4):
+        part = pl.ds(16 * r, 16)
+        head = [x_ref[part, pl.ds(16 * l, 16), :].astype(F32) for l in range(4)]
+        rest = dot(spread_tail, x_ref[part, pl.ds(64, 16), :].reshape(256, 128))
+        for f in range(2):
+            for l in range(4):
+                cut = pl.ds(128 * l, 128)
+                add = head[l][:, 8 * f : 8 * f + 8].reshape(128, 128)
+                old = latent_ref[f, r, pl.ds(0, 128), cut].astype(F32)
+                out[r, f, pl.ds(0, 128), cut] = (old + add).astype(BF)
+                at = 64 * l + 32 * f
+                old = latent_ref[f, r, pl.ds(128, 32), cut].astype(F32)
+                out[r, f, pl.ds(128, 32), cut] = (old + rest[at : at + 32]).astype(BF)
+        copies.append(pltpu.make_async_copy(out.at[r], out_any.at[:, r], sems.at[r]))
+        copies[r].start()
+    for copy in copies:
+        copy.wait()
 
 
 def finish(returned, latents):
-    block = pl.BlockSpec((2, 1, COLS, CH), lambda r: (0, r, 0, 0))
     return pl.pallas_call(
         finish_kernel,
         out_shape=jax.ShapeDtypeStruct(latents.shape, BF),
-        grid=(4,),
-        in_specs=[pl.BlockSpec((16, 80, 128), lambda r: (r, 0, 0)), block],
-        out_specs=block,
+        in_specs=[VMEM, VMEM],
+        out_specs=ANY,
+        scratch_shapes=[pltpu.VMEM((4, 2, COLS, CH), BF), pltpu.SemaphoreType.DMA((4,))],
         compiler_params=PARAMS,
         name="finish",
     )(returned, latents)

time: 119 us -> 117 us (0.983)
  Pallas kernels: 24.6 us -> 21.6 us
    pallas_call x1, Pallas kernels: 2.76 us -> 1.35 us  [finish(): pl.pallas_call(finish_kernel, out_shape=jax.ShapeDtypeStruct(latents.shap...]
  transfers between devices with their start and end apart: 3 -> 3, of which waited for: 2 -> 2; matrix products, arithmetic and copies ran while one was open for 0% -> 0% of each run, Pallas kernels for 7% -> 6%
where the time goes in v1:
time: 117 us; the launch traced here: 116 us
  blocking collectives  39.7 us (34%)
  waiting for transfers between devices  34.9 us (30%)
  Pallas kernels  21.6 us (18%)
  starting transfers between devices  18 us (15%)
  local copies, waits for them, and re-layouts  1.34 us (1%)
    all_to_all x1, blocking collectives, on_device(): lax.all_to_all(result, FRAME, split_axis=0, concat_axis=0, tiled=True)  39.7 us
    all_to_all x1, waiting for transfers between devices, on_device(): lax.all_to_all(payload, FRAME, split_axis=0, concat_axis=0, tiled=True)  33.7 us
    all_to_all x1, starting transfers between devices, on_device(): lax.all_to_all(payload, FRAME, split_axis=0, concat_axis=0, tiled=True)  12.1 us
    pallas_call x1, Pallas kernels, middle(): pl.pallas_call(middle_kernel, out_shape=jax.ShapeDtypeStruct((64, 80, 128...  10.3 us
    pallas_call x1, Pallas kernels, conv(): pl.pallas_call(conv_inner_kernel, out_shape=(payload, jax.ShapeDtypeStruc...  7.49 us
    ppermute x1, starting transfers between devices, on_device(): low = lax.ppermute(latents[:, 3:], 'slab', forward)  3.48 us
    pallas_call x1, Pallas kernels, conv(): pl.pallas_call(conv_edge_kernel, out_shape=payload, in_specs=[VMEM, VMEM,...  2.45 us
    ppermute x1, starting transfers between devices, on_device(): high = lax.ppermute(latents[:, :1], 'slab', backward)  2.37 us
  transfers between devices with their start and end apart: 3, of which 2 were waited for; matrix products, arithmetic and copies ran while one was open for 0% of the time, Pallas kernels for 6%

profile of v1, /device:TPU:8, one launch (start us, length us, event | category | flops | bytes accessed | tf_op | source)
XLA Modules:
  0.0 116.3 jit_solution(17612228468683472656)
XLA Ops:
  0.0 0.0 copy-start
  0.0 1.2 %fusion.1 = (bf16[2,1,160,512]{3,2,1,0:T(8,128)(2,1)S(1)}, bf16[2,1,160,512]{3,2,1,0:T(8,128)(2,1)S(1)}) fusion(bf16[2,4,160,512]{3,2,1,0:T(8,128)(2,1)} %latent_ref.1), kind=kLoop, calls=%fused_computation.12 | loop fusion | bytes 1310720 | tf_op jit(solution)/shard_map/slice | solution.py:374
  1.2 3.5 %collective-permute-start = (bf16[2,1,160,512]{3,2,1,0:T(8,128)(2,1)S(1)}, bf16[2,1,160,512]{3,2,1,0:T(8,128)(2,1)S(1)}, u32[]{:S(2)}, u32[]{:S(2)}) collective-permute-start(bf16[2,1,160,512]{3,2,1,0:T(8,128)(2,1)S(1)} %get-tuple-element.12), channel_id=1, source_target_pairs={{0,1},{1,2},{2,3},{4,5},{5,6},{6,7},{8,9},{9,10},{10,11},{12,13},{... | collective-permute-start | bytes 983048 | tf_op jit(solution)/shard_map/ppermute | solution.py:373
  4.7 2.4 %collective-permute-start.1 = (bf16[2,1,160,512]{3,2,1,0:T(8,128)(2,1)S(1)}, bf16[2,1,160,512]{3,2,1,0:T(8,128)(2,1)S(1)}, u32[]{:S(2)}, u32[]{:S(2)}) collective-permute-start(bf16[2,1,160,512]{3,2,1,0:T(8,128)(2,1)S(1)} %get-tuple-element.11), channel_id=1, source_target_pairs={{1,0},{2,1},{3,2},{5,4},{6,5},{7,6},{9,8},{10,9},{11,10},{13,12},{... | collective-permute-start | bytes 983048 | tf_op jit(solution)/shard_map/ppermute | solution.py:374
  7.1 0.0 copy-done
  7.1 7.5 %conv_inner.1 = (bf16[64,80,128]{2,1,0:T(8,128)(2,1)}, f32[2,320,512]{2,1,0:T(8,128)S(1)}, bf16[2,1536,512]{2,1,0:T(8,128)(2,1)S(1)}) custom-call(bf16[2,4,160,512]{3,2,1,0:T(8,128)(2,1)S(1)} %copy-done, bf16[3,1536,512]{2,1,0:T(8,128)(2,1)} %bitcast.5), custom_call_target="tpu_custom_call" | custom-call | flops 5033164800 | bytes 10485760 | tf_op jit(solution)/shard_map/conv_inner/pallas_call | solution.py:168
  14.6 0.0 collective-permute-done.low_ref
  14.6 1.2 collective-permute-done.1.high_ref
  15.8 2.5 %conv_edge.1 = bf16[64,80,128]{2,1,0:T(8,128)(2,1)} custom-call(bf16[2,1,160,512]{3,2,1,0:T(8,128)(2,1)S(1)} %collective-permute-done.low_ref, bf16[2,1,160,512]{3,2,1,0:T(8,128)(2,1)S(1)} %collective-permute-done.1.high_ref, f32[2,320,512]{2,1,0:T(8,128)S(1)} %get-tuple-element.8.edge_ref, ...), custom_call_target="tpu_custom_call", output_to_operand_aliasing={{}: (4, {})} | custom-call | tf_op jit(solution)/shard_map/conv_edge/pallas_call | solution.py:191
  18.2 0.0 copy-start.1
  18.3 12.1 %all-to-all-start = ((bf16[64,80,128]{2,1,0:T(8,128)(2,1)}), bf16[64,80,128]{2,1,0:T(8,128)(2,1)S(1)}, u32[]{:S(2)}, u32[]{:S(2)}) async-start(bf16[64,80,128]{2,1,0:T(8,128)(2,1)} %conv_edge.1), calls=%async_computation | async-start | bytes 2621440 | tf_op jit(solution)/shard_map/all_to_all | solution.py:376
  30.4 0.0 copy-done.1
  30.4 0.1 copy.9
  30.5 0.2 reduce-window.8
  30.7 0.1 reduce
  30.8 0.1 fusion
  31.0 33.7 %all-to-all-done.x_ref = bf16[64,80,128]{2,1,0:T(8,128)(2,1)S(1)} async-done(((bf16[64,80,128]{2,1,0:T(8,128)(2,1)}), bf16[64,80,128]{2,1,0:T(8,128)(2,1)S(1)}, u32[]{:S(2)}, u32[]{:S(2)}) %all-to-all-start) | async-done | bytes 1310752 | tf_op jit(solution)/shard_map/all_to_all | solution.py:376
  64.7 10.3 %middle.1 = bf16[64,80,128]{2,1,0:T(8,128)(2,1)S(1)} custom-call(bf16[64,80,128]{2,1,0:T(8,128)(2,1)S(1)} %all-to-all-done.x_ref, bf16[256,128]{1,0:T(8,128)(2,1)S(1)} %pad_maximum_fusion.shift_ref, f32[128,128]{1,0:T(8,128)S(1)} %get-tuple-element.13.bias_ref, bf16[1536,512]{1,0:T(8,128)(2,1)} %bitcast.3, bf16[512,1536]{1,0:T(8,128)(2,1)} %wq_any.1, ...), custom_call_target="tpu_custom_call" | custom-call | tf_op jit(solution)/shard_map/middle/pallas_call | solution.py:313
  75.0 39.7 %all_to_all.10.x_ref = bf16[64,80,128]{2,1,0:T(8,128)(2,1)S(1)} all-to-all(bf16[64,80,128]{2,1,0:T(8,128)(2,1)S(1)} %middle.1), channel_id=1, replica_groups=mesh['frame_0'=8,'frame_1'=4,'frame_2'=2,'slab'=4] {'frame_0','frame_1',..., dimensions={0} | all-to-all | bytes 2621440 | tf_op jit(solution)/shard_map/all_to_all | solution.py:378
  114.8 1.4 %finish.1 = bf16[2,4,160,512]{3,2,1,0:T(8,128)(2,1)} custom-call(bf16[64,80,128]{2,1,0:T(8,128)(2,1)S(1)} %all_to_all.10.x_ref, bf16[2,4,160,512]{3,2,1,0:T(8,128)(2,1)S(1)} %copy-done), custom_call_target="tpu_custom_call" | custom-call | tf_op jit(solution)/shard_map/finish/pallas_call | solution.py:358
  (2 shorter events, 0.0 us)
Async XLA Ops:
  0.0 7.1 %copy-start = (bf16[2,4,160,512]{3,2,1,0:T(8,128)(2,1)S(1)}, bf16[2,4,160,512]{3,2,1,0:T(8,128)(2,1)}, u32[]{:S(2)}) copy-start(bf16[2,4,160,512]{3,2,1,0:T(8,128)(2,1)} %latent_ref.1) | copy-start | bytes 3932164
  1.2 13.4 %collective-permute-start = (bf16[2,1,160,512]{3,2,1,0:T(8,128)(2,1)S(1)}, bf16[2,1,160,512]{3,2,1,0:T(8,128)(2,1)S(1)}, u32[]{:S(2)}, u32[]{:S(2)}) collective-permute-start(bf16[2,1,160,512]{3,2,1,0:T(8,128)(2,1)S(1)} %get-tuple-element.12), channel_id=1, source_target_pairs={{0,1},{1,2},{2,3},{4,5},{5,6},{6,7},{8,9},{9,10},{10,11},{12,13},{... | collective-permute-start | bytes 983048 | tf_op jit(solution)/shard_map/ppermute | solution.py:373
  4.7 11.1 %collective-permute-start.1 = (bf16[2,1,160,512]{3,2,1,0:T(8,128)(2,1)S(1)}, bf16[2,1,160,512]{3,2,1,0:T(8,128)(2,1)S(1)}, u32[]{:S(2)}, u32[]{:S(2)}) collective-permute-start(bf16[2,1,160,512]{3,2,1,0:T(8,128)(2,1)S(1)} %get-tuple-element.11), channel_id=1, source_target_pairs={{1,0},{2,1},{3,2},{5,4},{6,5},{7,6},{9,8},{10,9},{11,10},{13,12},{... | collective-permute-start | bytes 983048 | tf_op jit(solution)/shard_map/ppermute | solution.py:374
  18.2 12.1 %copy-start.1 = (s32[128]{0:T(128)S(1)}, s32[128]{0:T(128)}, u32[]{:S(2)}) copy-start(s32[128]{0:T(128)} %param.7) | copy-start | bytes 1540
  18.3 46.4 %all-to-all-start = ((bf16[64,80,128]{2,1,0:T(8,128)(2,1)}), bf16[64,80,128]{2,1,0:T(8,128)(2,1)S(1)}, u32[]{:S(2)}, u32[]{:S(2)}) async-start(bf16[64,80,128]{2,1,0:T(8,128)(2,1)} %conv_edge.1), calls=%async_computation | async-start | bytes 2621440 | tf_op jit(solution)/shard_map/all_to_all | solution.py:376

commit v2 on v1

--- a/solution.py
+++ b/solution.py
@@ -140,11 +140,13 @@
     copy.wait()
 
 
-def conv_edge_kernel(low_ref, high_ref, edge_ref, w_ref, held_ref, out_ref, xs, pay, sem):
+def conv_edge_kernel(first_ref, second_ref, edge_ref, w_ref, held_ref, out_ref, xs, pay, sem):
     del held_ref
+    even = lax.axis_index("slab") % 2 == 0
     for f in range(2):
-        spread_into(xs, f * COLS, low_ref[f, 0])
-        spread_into(xs, PAIR + f * COLS, high_ref[f, 0])
+        first, second = first_ref[f, 0].astype(F32), second_ref[f, 0].astype(F32)
+        spread_into(xs, f * COLS, jnp.where(even, second, first).astype(BF))
+        spread_into(xs, PAIR + f * COLS, jnp.where(even, first, second).astype(BF))
     tail = tail_matrix()
     copies = []
     for n in range(2):
@@ -162,7 +164,7 @@
         copy.wait()
 
 
-def conv(latents, low, high, w_space):
+def conv(latents, first, second, w_space):
     taps = far(w_space.reshape(3, 3 * CH, CH))
     payload = jax.ShapeDtypeStruct((64, 80, 128), BF)
     started, edge, outer = pl.pallas_call(
@@ -201,7 +203,7 @@
         input_output_aliases={4: 0},
         compiler_params=PARAMS,
         name="conv_edge",
-    )(low, high, edge, outer, started)
+    )(first, second, edge, outer, started)
 
 
 def gather_a(i):
@@ -249,10 +251,12 @@
         xs[pl.ds(k * TOTAL, TOTAL), pl.ds(CH, CH)] = moved[:TOTAL]
         xs[pl.ds(k * TOTAL, TOTAL), pl.ds(2 * CH, CH)] = moved[TOTAL:]
     weights[0].wait()
+    for c in range(2):
+        part = pl.ds(640 * c, 640)
+        mixed[part, :] = dot(xs[part, :], wt_ref[...]).astype(BF)
     weights[1].wait()
     for c in range(2):
         part = pl.ds(640 * c, 640)
-        mixed[part, :] = dot(xs[part, :], wt_ref[...]).astype(BF)
         for t in range(3):
             cut = pl.ds(t * CH, CH)
             qkv[part, cut] = dot(mixed[part, :], wq_ref[:, cut]).astype(BF)
@@ -366,13 +370,17 @@
     )(returned, latents)
 
 
+def swap(x, lower):
+    return lax.ppermute(x, "slab", [p for i in lower for p in ((i, i + 1), (i + 1, i))])
+
+
 def on_device(latents, clip_starts, w_space, w_time, w_qkv, w_out):
     count = lax.axis_size("slab")
-    forward = [(i, i + 1) for i in range(count - 1)]
-    backward = [(target, source) for source, target in forward]
-    low = lax.ppermute(latents[:, 3:], "slab", forward)
-    high = lax.ppermute(latents[:, :1], "slab", backward)
-    payload = conv(latents, low, high, w_space)
+    even = lax.axis_index("slab") % 2 == 0
+    top, bottom = latents[:, :1], latents[:, 3:]
+    first = swap(jnp.where(even, bottom, top), range(0, count - 1, 2))
+    second = swap(jnp.where(even, top, bottom), range(1, count - 1, 2))
+    payload = conv(latents, first, second, w_space)
     arrived = lax.all_to_all(payload, FRAME, split_axis=0, concat_axis=0, tiled=True)
     result = middle(arrived, clip_starts, w_time, w_qkv, w_out)
     returned = lax.all_to_all(result, FRAME, split_axis=0, concat_axis=0, tiled=True)

time: 117 us -> 114 us (0.974)
  local copies, waits for them, and re-layouts: 1.34 us -> 0.12 us
  other arithmetic: 0.41 us -> 1.63 us
  waiting for transfers between devices: 34.9 us -> 33.7 us
    select_n x0 -> x1, other arithmetic: none -> 1.22 us  [on_device(): second = swap(jnp.where(even, top, bottom), range(1, count - 1, 2))]
    slice x1 -> x0, local copies, waits for them, and re-layouts: 1.22 us -> none  [on_device(): high = lax.ppermute(latents[:, :1], 'slab', backward)]
  transfers between devices with their start and end apart: 3 -> 3, of which waited for: 2 -> 1; matrix products, arithmetic and copies ran while one was open for 0% -> 0% of each run, Pallas kernels for 6% -> 7%
where the time goes in v2:
time: 114 us
  blocking collectives  39.8 us (35%)
  waiting for transfers between devices  33.7 us (30%)
  Pallas kernels  21.4 us (19%)
  starting transfers between devices  17 us (15%)
  other arithmetic  1.63 us (1%)
    all_to_all x1, blocking collectives, on_device(): lax.all_to_all(result, FRAME, split_axis=0, concat_axis=0, tiled=True)  39.8 us
    all_to_all x1, waiting for transfers between devices, on_device(): lax.all_to_all(payload, FRAME, split_axis=0, concat_axis=0, tiled=True)  33.7 us
    all_to_all x1, starting transfers between devices, on_device(): lax.all_to_all(payload, FRAME, split_axis=0, concat_axis=0, tiled=True)  12.1 us
    pallas_call x1, Pallas kernels, middle(): pl.pallas_call(middle_kernel, out_shape=jax.ShapeDtypeStruct((64, 80, 128...  10 us
    pallas_call x1, Pallas kernels, conv(): pl.pallas_call(conv_inner_kernel, out_shape=(payload, jax.ShapeDtypeStruc...  7.48 us
    ppermute x2, starting transfers between devices, swap(): lax.ppermute(x, 'slab', [p for i in lower for p in ((i, i + 1), (i + 1, i...  4.84 us
    pallas_call x1, Pallas kernels, conv(): pl.pallas_call(conv_edge_kernel, out_shape=payload, in_specs=[VMEM, VMEM,...  2.56 us
  transfers between devices with their start and end apart: 3, of which 1 were waited for; matrix products, arithmetic and copies ran while one was open for 0% of the time, Pallas kernels for 7%

profile of v2, /device:TPU:8, one launch (start us, length us, event | category | flops | bytes accessed | tf_op | source)
XLA Modules:
  0.0 113.9 jit_solution(2540623674138072111)
XLA Ops:
  0.0 0.0 copy-start
  0.0 1.2 %broadcast_select_fusion = (bf16[2,1,160,512]{3,2,1,0:T(8,128)(2,1)S(1)}, bf16[2,1,160,512]{3,2,1,0:T(8,128)(2,1)S(1)}) fusion(pred[]{:T(512)S(6)} %eq.24, bf16[2,4,160,512]{3,2,1,0:T(8,128)(2,1)} %latent_ref.1), kind=kLoop, calls=%fused_computation | loop fusion | flops 327680 | bytes 1310721 | tf_op jit(solution)/shard_map/jit(_where)/select_n | solution.py:382
  1.2 2.2 %collective-permute-start = (bf16[2,1,160,512]{3,2,1,0:T(8,128)(2,1)S(1)}, bf16[2,1,160,512]{3,2,1,0:T(8,128)(2,1)S(1)}, u32[]{:S(2)}, u32[]{:S(2)}) collective-permute-start(bf16[2,1,160,512]{3,2,1,0:T(8,128)(2,1)S(1)} %get-tuple-element.12), channel_id=1, source_target_pairs={{0,1},{1,0},{2,3},{3,2},{4,5},{5,4},{6,7},{7,6},{8,9},{9,8},{10,11... | collective-permute-start | bytes 983048 | tf_op jit(solution)/shard_map/ppermute | solution.py:374
  3.5 2.6 %collective-permute-start.1 = (bf16[2,1,160,512]{3,2,1,0:T(8,128)(2,1)S(1)}, bf16[2,1,160,512]{3,2,1,0:T(8,128)(2,1)S(1)}, u32[]{:S(2)}, u32[]{:S(2)}) collective-permute-start(bf16[2,1,160,512]{3,2,1,0:T(8,128)(2,1)S(1)} %get-tuple-element.11), channel_id=1, source_target_pairs={{1,2},{2,1},{5,6},{6,5},{9,10},{10,9},{13,14},{14,13},{17,18},{18,... | collective-permute-start | bytes 983048 | tf_op jit(solution)/shard_map/ppermute | solution.py:374
  6.1 0.0 copy-done
  6.1 7.5 %conv_inner.1 = (bf16[64,80,128]{2,1,0:T(8,128)(2,1)}, f32[2,320,512]{2,1,0:T(8,128)S(1)}, bf16[2,1536,512]{2,1,0:T(8,128)(2,1)S(1)}) custom-call(bf16[2,4,160,512]{3,2,1,0:T(8,128)(2,1)S(1)} %copy-done, bf16[3,1536,512]{2,1,0:T(8,128)(2,1)} %bitcast.5), custom_call_target="tpu_custom_call" | custom-call | flops 5033164800 | bytes 10485760 | tf_op jit(solution)/shard_map/conv_inner/pallas_call | solution.py:170
  13.6 0.0 collective-permute-done.first_ref
  13.6 0.0 collective-permute-done.1.second_ref
  13.6 2.6 %conv_edge.1 = bf16[64,80,128]{2,1,0:T(8,128)(2,1)} custom-call(bf16[2,1,160,512]{3,2,1,0:T(8,128)(2,1)S(1)} %collective-permute-done.first_ref, bf16[2,1,160,512]{3,2,1,0:T(8,128)(2,1)S(1)} %collective-permute-done.1.second_ref, f32[2,320,512]{2,1,0:T(8,128)S(1)} %get-tuple-element.8.edge_ref, ...), custom_call_target="tpu_custom_call", output_to_operand_aliasing={{}: (4, {})} | custom-call | tf_op jit(solution)/shard_map/conv_edge/pallas_call | solution.py:193
  16.2 0.0 copy-start.1
  16.2 12.1 %all-to-all-start = ((bf16[64,80,128]{2,1,0:T(8,128)(2,1)}), bf16[64,80,128]{2,1,0:T(8,128)(2,1)S(1)}, u32[]{:S(2)}, u32[]{:S(2)}) async-start(bf16[64,80,128]{2,1,0:T(8,128)(2,1)} %conv_edge.1), calls=%async_computation | async-start | bytes 2621440 | tf_op jit(solution)/shard_map/all_to_all | solution.py:384
  28.3 0.0 copy-done.1
  28.3 0.1 copy.9
  28.4 0.2 reduce-window.8
  28.6 0.1 reduce
  28.7 0.1 fusion
  28.9 33.7 %all-to-all-done.x_ref = bf16[64,80,128]{2,1,0:T(8,128)(2,1)S(1)} async-done(((bf16[64,80,128]{2,1,0:T(8,128)(2,1)}), bf16[64,80,128]{2,1,0:T(8,128)(2,1)S(1)}, u32[]{:S(2)}, u32[]{:S(2)}) %all-to-all-start) | async-done | bytes 1310752 | tf_op jit(solution)/shard_map/all_to_all | solution.py:384
  62.6 10.0 %middle.1 = bf16[64,80,128]{2,1,0:T(8,128)(2,1)S(1)} custom-call(bf16[64,80,128]{2,1,0:T(8,128)(2,1)S(1)} %all-to-all-done.x_ref, bf16[256,128]{1,0:T(8,128)(2,1)S(1)} %pad_maximum_fusion.shift_ref, f32[128,128]{1,0:T(8,128)S(1)} %get-tuple-element.13.bias_ref, bf16[1536,512]{1,0:T(8,128)(2,1)} %bitcast.3, bf16[512,1536]{1,0:T(8,128)(2,1)} %wq_any.1, ...), custom_call_target="tpu_custom_call" | custom-call | tf_op jit(solution)/shard_map/middle/pallas_call | solution.py:317
  72.6 39.8 %all_to_all.10.x_ref = bf16[64,80,128]{2,1,0:T(8,128)(2,1)S(1)} all-to-all(bf16[64,80,128]{2,1,0:T(8,128)(2,1)S(1)} %middle.1), channel_id=1, replica_groups=mesh['frame_0'=8,'frame_1'=4,'frame_2'=2,'slab'=4] {'frame_0','frame_1',..., dimensions={0} | all-to-all | bytes 2621440 | tf_op jit(solution)/shard_map/all_to_all | solution.py:386
  112.4 1.4 %finish.1 = bf16[2,4,160,512]{3,2,1,0:T(8,128)(2,1)} custom-call(bf16[64,80,128]{2,1,0:T(8,128)(2,1)S(1)} %all_to_all.10.x_ref, bf16[2,4,160,512]{3,2,1,0:T(8,128)(2,1)S(1)} %copy-done), custom_call_target="tpu_custom_call" | custom-call | tf_op jit(solution)/shard_map/finish/pallas_call | solution.py:362
  (2 shorter events, 0.0 us)
Async XLA Ops:
  0.0 6.1 %copy-start = (bf16[2,4,160,512]{3,2,1,0:T(8,128)(2,1)S(1)}, bf16[2,4,160,512]{3,2,1,0:T(8,128)(2,1)}, u32[]{:S(2)}) copy-start(bf16[2,4,160,512]{3,2,1,0:T(8,128)(2,1)} %latent_ref.1) | copy-start | bytes 3932164
  1.2 12.4 %collective-permute-start = (bf16[2,1,160,512]{3,2,1,0:T(8,128)(2,1)S(1)}, bf16[2,1,160,512]{3,2,1,0:T(8,128)(2,1)S(1)}, u32[]{:S(2)}, u32[]{:S(2)}) collective-permute-start(bf16[2,1,160,512]{3,2,1,0:T(8,128)(2,1)S(1)} %get-tuple-element.12), channel_id=1, source_target_pairs={{0,1},{1,0},{2,3},{3,2},{4,5},{5,4},{6,7},{7,6},{8,9},{9,8},{10,11... | collective-permute-start | bytes 983048 | tf_op jit(solution)/shard_map/ppermute | solution.py:374
  3.5 10.1 %collective-permute-start.1 = (bf16[2,1,160,512]{3,2,1,0:T(8,128)(2,1)S(1)}, bf16[2,1,160,512]{3,2,1,0:T(8,128)(2,1)S(1)}, u32[]{:S(2)}, u32[]{:S(2)}) collective-permute-start(bf16[2,1,160,512]{3,2,1,0:T(8,128)(2,1)S(1)} %get-tuple-element.11), channel_id=1, source_target_pairs={{1,2},{2,1},{5,6},{6,5},{9,10},{10,9},{13,14},{14,13},{17,18},{18,... | collective-permute-start | bytes 983048 | tf_op jit(solution)/shard_map/ppermute | solution.py:374
  16.2 12.2 %copy-start.1 = (s32[128]{0:T(128)S(1)}, s32[128]{0:T(128)}, u32[]{:S(2)}) copy-start(s32[128]{0:T(128)} %param.7) | copy-start | bytes 1540
  16.2 46.4 %all-to-all-start = ((bf16[64,80,128]{2,1,0:T(8,128)(2,1)}), bf16[64,80,128]{2,1,0:T(8,128)(2,1)S(1)}, u32[]{:S(2)}, u32[]{:S(2)}) async-start(bf16[64,80,128]{2,1,0:T(8,128)(2,1)} %conv_edge.1), calls=%async_computation | async-start | bytes 2621440 | tf_op jit(solution)/shard_map/all_to_all | solution.py:384
